TPU v7x, 32 devices: a whole 2x2x4 slice. The times are simulated.
32 devices in a mesh: section: 2 (over core), table: 16 (over z, y, x).
Axes of the slice: x: 2, y: 2, z: 4, core: 2. Of those that a mesh axis runs over, the one named last changes fastest.
Arguments:
- gate_a: bfloat16 [2, 1024, 4096], P('section', 'table'), may hold values from -6 to 6
- cotangent_a: bfloat16 [2, 1024, 4096], P('section', 'table'), may hold values from -6 to 6
- gate_b: bfloat16 [2, 1024, 4096], P('section', 'table'), may hold values from -6 to 6
- table: bfloat16 [1024, 4096], P('table'), may hold values from -6 to 6
- row_ids: int32 [2, 2, 16, 128], P('section', None, 'table'), may hold values from 0 to 1023, as said below
- slots: int32 [2, 2, 1024, 128], P('section', None, 'table'), may hold values from 0 to 127, as said below
- weights: float32 [2, 2, 1024, 128], P('section', None, 'table'), may hold values from 0.02 to 0.2
Outputs:
- mixed_b: bfloat16 [2, 1024, 4096], P('section', 'table')
- grad_gate_a: bfloat16 [2, 1024, 4096], P('section', 'table')
- grad_weights_a: float32 [2, 1024, 128], P('section', 'table')
- grad_table: float32 [1024, 4096], P('table', 'section')
Inputs may be any that keep to these rules, and one draw needn't show every extreme that they name: `row_ids`: row r is held by index r // 64 of table. The 128 ids of one list are distinct, and at most 8 of them are held by one index of table; in every section and micro-batch some index of table holds 8 ids of every device's list. `slots`: the 32 picks of one token and head are distinct, and every position of a device's list is picked by some token of that device and micro-batch.
All inputs are finite; a program needn't handle non-finite values.
Results may differ from a plain program's by a relative error of at most 0.0057.
Values may be sent and summed in bfloat16 or wider, within the bound.
A program may use at most 128 MiB of HBM per device.

v0:
```python
import jax
import jax.numpy as jnp
from jax import lax
from jax.sharding import PartitionSpec as P

ROW_LIMIT = 8


def bucket_rows(row_list, rows_dev, owners, capacity):
    owner_of = row_list // rows_dev
    offset = row_list - owner_of * rows_dev
    member = (owner_of[:, None] == jnp.arange(owners, dtype=jnp.int32)[None, :]).astype(jnp.int32)
    earlier = jnp.cumsum(member, axis=0) - member
    position = jnp.sum(earlier * member, axis=1)
    slot_place = owner_of * capacity + position
    requests = jnp.full((owners * capacity,), -1, jnp.int32).at[slot_place].set(offset)
    return (requests.reshape(owners, capacity), slot_place)


def combine_table(slot_rows, weight_rows, listed):
    matches = slot_rows[:, :, None] == jnp.arange(listed, dtype=jnp.int32)[None, None, :]
    return jnp.sum(
        jnp.where(matches, weight_rows[:, :, None], jnp.zeros_like(weight_rows[:, :, None])), axis=1
    ).astype(jnp.bfloat16)


def local(gate_a, cotangent_a, gate_b, table, row_ids, slots, weights):
    owners = lax.axis_size("table")
    rows_dev = table.shape[0]
    features = table.shape[1]
    listed = row_ids.shape[-1]
    requests_a, place_a = bucket_rows(row_ids[0, 0, 0], rows_dev, owners, ROW_LIMIT)
    requests_b, place_b = bucket_rows(row_ids[0, 1, 0], rows_dev, owners, ROW_LIMIT)

    def serve_rows(received):
        present = received >= 0
        picked = jnp.take(table, jnp.maximum(received, 0), axis=0)
        return jnp.where(present[..., None], picked, jnp.zeros_like(picked))

    def serve_one(received):
        return (
            lax.all_to_all(serve_rows(received), "table", split_axis=0, concat_axis=0, tiled=True),
            received,
        )

    def fetch_list(requests):
        return serve_one(lax.all_to_all(requests, "table", split_axis=0, concat_axis=0, tiled=True))

    fetched_a, kept_a = fetch_list(requests_a)
    fetched_rows = fetched_a.reshape(-1, features)[place_a]
    mixing = combine_table(slots[0, 0], weights[0, 0], listed)
    memory = jnp.dot(mixing, fetched_rows, preferred_element_type=jnp.float32)
    gate_value = gate_a[0].astype(jnp.float32)
    incoming = cotangent_a[0].astype(jnp.float32)
    logistic = jax.nn.sigmoid(gate_value)
    grad_gate = (incoming * memory * logistic * (1.0 + gate_value * (1.0 - logistic))).astype(
        jnp.bfloat16
    )
    grad_memory = (incoming * gate_value * logistic).astype(jnp.bfloat16)
    row_scores = lax.dot_general(
        grad_memory, fetched_rows, (((1,), (1,)), ((), ())), preferred_element_type=jnp.float32
    )
    grad_weights = jnp.take_along_axis(row_scores, slots[0, 0], axis=1)
    grad_rows = lax.dot_general(
        mixing, grad_memory, (((0,), (0,)), ((), ())), preferred_element_type=jnp.float32
    ).astype(jnp.bfloat16)
    outgoing = (
        jnp.zeros((owners * ROW_LIMIT, features), jnp.bfloat16)
        .at[place_a]
        .set(grad_rows)
        .reshape(owners, ROW_LIMIT, features)
    )
    arrived = lax.all_to_all(outgoing, "table", split_axis=0, concat_axis=0, tiled=True)
    owner_match = (kept_a.reshape(1, -1) == jnp.arange(rows_dev, dtype=jnp.int32)[:, None]).astype(
        jnp.bfloat16
    )
    owner_sum = jnp.dot(
        owner_match, arrived.reshape(-1, features), preferred_element_type=jnp.float32
    )
    grad_table = lax.psum_scatter(owner_sum, "section", scatter_dimension=1, tiled=True)
    grad_gate_a, grad_weights_a, grad_table = (grad_gate[None], grad_weights[None], grad_table)
    fetched_b, kept_b = fetch_list(requests_b)
    fetched_rows = fetched_b.reshape(-1, features)[place_b]
    mixing = combine_table(slots[0, 1], weights[0, 1], listed)
    memory = jnp.dot(mixing, fetched_rows, preferred_element_type=jnp.float32)
    gate_value = gate_b[0].astype(jnp.float32)
    mixed_b = (gate_value * jax.nn.sigmoid(gate_value) * memory).astype(jnp.bfloat16)[None]
    return (mixed_b, grad_gate_a, grad_weights_a, grad_table)


def solution(mesh):
    return jax.shard_map(
        local,
        mesh=mesh,
        in_specs=(
            P("section", "table", None),
            P("section", "table", None),
            P("section", "table", None),
            P("table", None),
            P("section", None, "table", None),
            P("section", None, "table", None),
            P("section", None, "table", None),
        ),
        out_specs=(
            P("section", "table", None),
            P("section", "table", None),
            P("section", "table", None),
            P("table", "section"),
        ),
        check_vma=False,
    )
```

profile of v0, /device:TPU:15, one launch (start us, length us, event | category | flops | bytes accessed | tf_op | source)
XLA Modules:
  0.0 187.9 jit_solution(11483915157261362422)
XLA Ops:
  7.2 0.0 copy-start
  7.2 0.0 copy-start.2
  7.2 0.8 bitcast_subtract_fusion
  8.0 0.1 fusion.21
  8.1 0.1 fusion.22
  8.1 0.2 reduce_window_sum.18
  8.3 0.2 reduce_window_sum.17
  8.5 0.2 select_reduce_fusion.2
  8.7 0.7 fusion.32
  9.4 1.0 scatter_custom_fusion
  10.3 0.7 all_to_all.21
  11.0 6.6 %all-to-all-start = ((s32[16,1,8]{2,1,0:T(1,128)}), s32[16,1,8]{2,1,0:T(1,128)S(1)}, u32[]{:S(2)}, u32[]{:S(2)}) async-start(s32[16,1,8]{2,1,0:T(1,128)} %bitcast.8), calls=%async_computation | async-start | bytes 16384 | tf_op jit(solution)/shard_map/all_to_all | solution.py:47
  17.6 0.8 slice_bitcast_fusion
  18.4 0.8 slice_bitcast_fusion.3
  19.2 0.0 copy-done.2
  19.2 1.3 fusion.14
  20.5 2.8 %select_reduce_fusion = bf16[64,128]{1,0:T(8,128)(2,1)S(1)} fusion(f32[64,128]{1,0:T(8,128)S(1)} %get-tuple-element.11, s32[64,128]{1,0:T(8,128)S(1)} %get-tuple-element.9), kind=kLoop, calls=%fused_computation.17 | loop fusion | flops 3137536 | bytes 81920 | tf_op jit(solution)/shard_map/reduce_sum | solution.py:22
  23.3 1.0 scatter_custom_fusion.1
  24.3 0.7 all_to_all.24
  25.0 0.0 all-to-all-done
  25.0 6.4 %all-to-all-start.2 = ((s32[16,1,8]{2,1,0:T(1,128)}), s32[16,1,8]{2,1,0:T(1,128)S(1)}, u32[]{:S(2)}, u32[]{:S(2)}) async-start(s32[16,1,8]{2,1,0:T(1,128)} %bitcast.21), calls=%async_computation.2 | async-start | bytes 16384 | tf_op jit(solution)/shard_map/all_to_all | solution.py:47
  31.3 0.4 convolution_convert_fusion
  31.8 3.1 %scatter_custom_fusion.2 = bf16[128,4096]{1,0:T(8,128)(2,1)} fusion(s32[128]{0:T(128)S(1)} %get-tuple-element.13, bf16[128,4096]{1,0:T(8,128)(2,1)S(1)} %convolution_convert_fusion, bf16[]{:T(256)} %constant.68.clone.1), kind=kCustom, calls=%fused_computation.41 | custom fusion | bytes 1048578 | tf_op jit(solution)/shard_map/scatter | solution.py:70
  34.8 0.0 all-to-all-done.2
  34.9 6.4 %all-to-all-start.4 = ((bf16[16,8,4096]{2,1,0:T(8,128)(2,1)}), bf16[16,8,4096]{2,1,0:T(8,128)(2,1)S(1)}, u32[]{:S(2)}, u32[]{:S(2)}) async-start(bf16[16,8,4096]{2,1,0:T(8,128)(2,1)} %bitcast.34), calls=%async_computation.4 | async-start | bytes 2097152 | tf_op jit(solution)/shard_map/all_to_all | solution.py:73
  41.2 0.1 copy.44
  41.3 0.1 copy.48
  41.4 0.1 reshape.414
  41.5 0.1 copy.47
  41.6 0.1 copy.45
  41.7 0.0 copy-done
  41.7 1.2 gather_fusion.3
  42.9 1.3 fusion.18
  44.1 21.1 %all-to-all-done.4 = bf16[16,8,4096]{2,1,0:T(8,128)(2,1)S(1)} async-done(((bf16[16,8,4096]{2,1,0:T(8,128)(2,1)}), bf16[16,8,4096]{2,1,0:T(8,128)(2,1)S(1)}, u32[]{:S(2)}, u32[]{:S(2)}) %all-to-all-start.4) | async-done | bytes 1048608 | tf_op jit(solution)/shard_map/all_to_all | solution.py:73
  65.2 1.0 copy-done.1
  66.2 4.9 %all-to-all-start.1 = ((bf16[16,8,4096]{2,1,0:T(8,128)(2,1)}), bf16[16,8,4096]{2,1,0:T(8,128)(2,1)S(1)}, u32[]{:S(2)}, u32[]{:S(2)}) async-start(bf16[16,8,4096]{2,1,0:T(8,128)(2,1)} %fusion.18), calls=%async_computation.1 | async-start | bytes 2097152 | tf_op jit(solution)/shard_map/all_to_all | solution.py:42
  71.1 0.1 copy.50
  71.2 0.1 copy.54
  71.3 0.1 reshape.418
  71.4 1.2 gather_fusion.4
  72.6 0.1 copy.53
  72.7 0.1 copy.51
  72.8 1.2 fusion.17
  74.0 21.1 %all-to-all-done.1 = bf16[16,8,4096]{2,1,0:T(8,128)(2,1)S(1)} async-done(((bf16[16,8,4096]{2,1,0:T(8,128)(2,1)}), bf16[16,8,4096]{2,1,0:T(8,128)(2,1)S(1)}, u32[]{:S(2)}, u32[]{:S(2)}) %all-to-all-start.1) | async-done | bytes 1048608 | tf_op jit(solution)/shard_map/all_to_all | solution.py:42
  95.1 4.9 %all-to-all-start.3 = ((bf16[16,8,4096]{2,1,0:T(8,128)(2,1)}), bf16[16,8,4096]{2,1,0:T(8,128)(2,1)S(1)}, u32[]{:S(2)}, u32[]{:S(2)}) async-start(bf16[16,8,4096]{2,1,0:T(8,128)(2,1)} %fusion.17), calls=%async_computation.3 | async-start | bytes 2097152 | tf_op jit(solution)/shard_map/all_to_all | solution.py:42
  100.1 0.0 reduce-scatter.2.cloned.1.call-start
  100.1 0.5 broadcast.357
  100.6 0.7 reduce.3
  101.3 0.1 eq.85
  101.4 2.6 %fusion.15 = f32[64,4096]{1,0:T(8,128)} fusion(bf16[16,8,4096]{2,1,0:T(8,128)(2,1)} %copy-done.1, s32[128]{0:T(128)S(1)} %eq.85), kind=kOutput, calls=%fused_computation.35 | convolution fusion | flops 67117056 | bytes 2097664 | tf_op jit(solution)/shard_map/dot_general | solution.py:77
  103.9 0.0 reduce-scatter.2.cloned.1.call-update
  104.0 2.8 %select_reduce_fusion.1 = bf16[64,128]{1,0:T(8,128)(2,1)S(1)} fusion(f32[64,128]{1,0:T(8,128)S(1)} %get-tuple-element.12, s32[64,128]{1,0:T(8,128)S(1)} %get-tuple-element.10), kind=kLoop, calls=%fused_computation.19 | loop fusion | flops 3137536 | bytes 81920 | tf_op jit(solution)/shard_map/reduce_sum | solution.py:22
  106.8 0.0 copy-done.5
  106.8 2.2 %gather_fusion = bf16[128,4096]{1,0:T(8,128)(2,1)} fusion(bf16[128,4096]{1,0:T(8,128)(2,1)S(1)} %bitcast.121, s32[1024]{0:T(1024)S(1)} %pad_clamp_fusion.2), kind=kCustom, calls=%fused_computation.2 | custom fusion | bytes 2097664 | tf_op jit(solution)/shard_map/gather | solution.py:83
  109.0 15.0 %all-to-all-done.3 = bf16[16,8,4096]{2,1,0:T(8,128)(2,1)S(1)} async-done(((bf16[16,8,4096]{2,1,0:T(8,128)(2,1)}), bf16[16,8,4096]{2,1,0:T(8,128)(2,1)S(1)}, u32[]{:S(2)}, u32[]{:S(2)}) %all-to-all-start.3) | async-done | bytes 1048608 | tf_op jit(solution)/shard_map/all_to_all | solution.py:42
  124.0 1.2 gather_fusion.1
  125.2 0.5 fusion.37
  125.7 0.0 copy-start.6
  125.7 50.7 %gather_fusion.2 = f32[8192]{0:T(1024)S(1)} fusion(f32[64,128]{1,0:T(8,128)S(1)} %fusion.37, s32[8192]{0:T(1024)S(1)} %fusion.26), kind=kCustom, calls=%fused_computation.4 | custom fusion | bytes 131072 | tf_op jit(solution)/shard_map/jit(take_along_axis)/gather | solution.py:63
  176.4 0.6 bitcast_select_fusion.2
  177.0 0.0 copy-done.6
  177.1 2.6 %fusion.4 = bf16[1,64,4096]{2,1,0:T(8,128)(2,1)} fusion(bf16[128,4096]{1,0:T(8,128)(2,1)} %gather_fusion, bf16[1,64,4096]{2,1,0:T(8,128)(2,1)S(1)} %copy-done.6, bf16[64,128]{1,0:T(8,128)(2,1)S(1)} %select_reduce_fusion.1), kind=kOutput, calls=%fused_computation.15 | convolution fusion | flops 68943872 | bytes 2113536 | tf_op jit(solution)/shard_map/dot_general | solution.py:85
  179.6 0.0 copy-done.4
  179.6 1.4 fusion.5
  (17 shorter events, 0.1 us)
Async XLA Ops:
  7.2 34.5 %copy-start = (bf16[64,4096]{1,0:T(8,128)(2,1)S(1)}, bf16[64,4096]{1,0:T(8,128)(2,1)}, u32[]{:S(2)}) copy-start(bf16[64,4096]{1,0:T(8,128)(2,1)} %param.12) | copy-start | bytes 1572868
  7.2 12.0 %copy-start.2 = (bf16[1,64,4096]{2,1,0:T(8,128)(2,1)S(1)}, bf16[1,64,4096]{2,1,0:T(8,128)(2,1)}, u32[]{:S(2)}) copy-start(bf16[1,64,4096]{2,1,0:T(8,128)(2,1)} %param.10) | copy-start | bytes 1572868
  11.0 14.0 %all-to-all-start = ((s32[16,1,8]{2,1,0:T(1,128)}), s32[16,1,8]{2,1,0:T(1,128)S(1)}, u32[]{:S(2)}, u32[]{:S(2)}) async-start(s32[16,1,8]{2,1,0:T(1,128)} %bitcast.8), calls=%async_computation | async-start | bytes 16384 | tf_op jit(solution)/shard_map/all_to_all | solution.py:47
  25.0 9.9 %all-to-all-start.2 = ((s32[16,1,8]{2,1,0:T(1,128)}), s32[16,1,8]{2,1,0:T(1,128)S(1)}, u32[]{:S(2)}, u32[]{:S(2)}) async-start(s32[16,1,8]{2,1,0:T(1,128)} %bitcast.21), calls=%async_computation.2 | async-start | bytes 16384 | tf_op jit(solution)/shard_map/all_to_all | solution.py:47
  34.9 30.4 %all-to-all-start.4 = ((bf16[16,8,4096]{2,1,0:T(8,128)(2,1)}), bf16[16,8,4096]{2,1,0:T(8,128)(2,1)S(1)}, u32[]{:S(2)}, u32[]{:S(2)}) async-start(bf16[16,8,4096]{2,1,0:T(8,128)(2,1)} %bitcast.34), calls=%async_computation.4 | async-start | bytes 2097152 | tf_op jit(solution)/shard_map/all_to_all | solution.py:73
  65.2 1.0 copy-start.1
  66.2 28.9 %all-to-all-start.1 = ((bf16[16,8,4096]{2,1,0:T(8,128)(2,1)}), bf16[16,8,4096]{2,1,0:T(8,128)(2,1)S(1)}, u32[]{:S(2)}, u32[]{:S(2)}) async-start(bf16[16,8,4096]{2,1,0:T(8,128)(2,1)} %fusion.18), calls=%async_computation.1 | async-start | bytes 2097152 | tf_op jit(solution)/shard_map/all_to_all | solution.py:42
  95.1 28.9 %all-to-all-start.3 = ((bf16[16,8,4096]{2,1,0:T(8,128)(2,1)}), bf16[16,8,4096]{2,1,0:T(8,128)(2,1)S(1)}, u32[]{:S(2)}, u32[]{:S(2)}) async-start(bf16[16,8,4096]{2,1,0:T(8,128)(2,1)} %fusion.17), calls=%async_computation.3 | async-start | bytes 2097152 | tf_op jit(solution)/shard_map/all_to_all | solution.py:42
  100.1 81.0 %reduce-scatter.2.cloned.1.call-start = ((), (), s32[]{:S(2)}) async-start(), calls=%async_computation.6 | async-start | bytes 1572864 | tf_op jit(solution)/shard_map/reduce_scatter | solution.py:80
  103.9 2.8 %copy-start.5 = (s32[1,2,64,128]{3,2,1,0:T(8,128)S(1)}, s32[1,2,64,128]{3,2,1,0:T(8,128)}, u32[]{:S(2)}) copy-start(s32[1,2,64,128]{3,2,1,0:T(8,128)} %param.14) | copy-start | bytes 196612
  125.7 51.3 %copy-start.6 = (bf16[1,64,4096]{2,1,0:T(8,128)(2,1)S(1)}, bf16[1,64,4096]{2,1,0:T(8,128)(2,1)}, u32[]{:S(2)}) copy-start(bf16[1,64,4096]{2,1,0:T(8,128)(2,1)} %param.11) | copy-start | bytes 1572868
  177.1 2.6 %copy-start.3 = (bf16[1,64,4096]{2,1,0:T(8,128)(2,1)S(1)}, bf16[1,64,4096]{2,1,0:T(8,128)(2,1)}, u32[]{:S(2)}) copy-start(bf16[1,64,4096]{2,1,0:T(8,128)(2,1)} %param.10) | copy-start | bytes 1572868
  177.1 2.6 %copy-start.4 = (bf16[1,64,4096]{2,1,0:T(8,128)(2,1)S(1)}, bf16[1,64,4096]{2,1,0:T(8,128)(2,1)}, u32[]{:S(2)}) copy-start(bf16[1,64,4096]{2,1,0:T(8,128)(2,1)} %param.9) | copy-start | bytes 1572868
Sparse Core Ops, SparseCore 0:
  104.1 12.0 reduce-scatter.1
where the time goes:
time: 191 us; the launch traced here: 188 us
  local copies, waits for them, and re-layouts  66.8 us (35%)
  waiting for transfers between devices  57.2 us (30%)
  starting transfers between devices  29.2 us (15%)
  between operations  14.2 us (7%)
  other arithmetic  12.9 us (7%)
  matrix products  7.45 us (4%)
    gather x1, local copies, waits for them, and re-layouts, local(): grad_weights = jnp.take_along_axis(row_scores, slots[0, 0], axis=1)  50.7 us
    all_to_all x2, waiting for transfers between devices, serve_one(): lax.all_to_all(serve_rows(received), 'table', split_axis=0, concat_axis=0...  36.2 us
    all_to_all x1, waiting for transfers between devices, local(): lax.all_to_all(outgoing, 'table', split_axis=0, concat_axis=0, tiled=True)  21.1 us
    all_to_all x2, starting transfers between devices, fetch_list(): lax.all_to_all(requests, 'table', split_axis=0, concat_axis=0, tiled=True)  12.9 us
    all_to_all x2, starting transfers between devices, serve_one(): lax.all_to_all(serve_rows(received), 'table', split_axis=0, concat_axis=0...  9.87 us
    all_to_all x1, starting transfers between devices, local(): lax.all_to_all(outgoing, 'table', split_axis=0, concat_axis=0, tiled=True)  6.37 us
    reduce_sum x2, other arithmetic, combine_table(): jnp.sum(jnp.where(matches, weight_rows[:, :, None], jnp.zeros_like(weight...  5.58 us
    dot_general x2, matrix products, local(): memory = jnp.dot(mixing, fetched_rows, preferred_element_type=jnp.float32)  3.96 us
  transfers between devices with their start and end apart: 6, of which 3 were waited for; matrix products, arithmetic and copies ran while one was open for 43% of the time, Pallas kernels for 0%

commit v1 on v0

v1 whole, which is shorter than its diff:
```python
import jax
import jax.numpy as jnp
from jax import lax
from jax.sharding import PartitionSpec as P

ROW_LIMIT = 8


def place_rows(row_list, rows_dev, owners, capacity):
    owner_of = row_list // rows_dev
    offset = row_list - owner_of * rows_dev
    listed = row_list.shape[0]
    same = owner_of[:, None] == owner_of[None, :]
    before = jnp.arange(listed)[None, :] < jnp.arange(listed)[:, None]
    position = jnp.sum((same & before).astype(jnp.int32), axis=1)
    place = owner_of * capacity + position
    permute = (place[:, None] == jnp.arange(owners * capacity, dtype=jnp.int32)[None, :])
    requests = jnp.max(jnp.where(permute, offset[:, None], -1), axis=0)
    return requests.reshape(owners, capacity), permute.astype(jnp.bfloat16)


def combine_table(slot_rows, weight_rows, listed):
    matches = slot_rows[:, :, None] == jnp.arange(listed, dtype=jnp.int32)[None, None, :]
    return jnp.sum(
        jnp.where(matches, weight_rows[:, :, None], jnp.zeros_like(weight_rows[:, :, None])), axis=1
    ).astype(jnp.bfloat16)


def local(gate_a, cotangent_a, gate_b, table, row_ids, slots, weights):
    owners = lax.axis_size("table")
    sections = lax.axis_size("section")
    rows_dev, features = table.shape
    listed = row_ids.shape[-1]
    part = features // sections
    requests_a, permute_a = place_rows(row_ids[0, 0, 0], rows_dev, owners, ROW_LIMIT)
    requests_b, permute_b = place_rows(row_ids[0, 1, 0], rows_dev, owners, ROW_LIMIT)
    requests = jnp.stack([requests_a, requests_b], axis=1)
    received = lax.all_to_all(requests, "table", split_axis=0, concat_axis=0, tiled=True)
    asked_a = lax.all_gather(received[:, 0].reshape(-1), "section", axis=0, tiled=True)
    row_index = jnp.arange(rows_dev, dtype=jnp.int32)

    def serve(wanted):
        picks = (wanted.reshape(-1)[:, None] == row_index[None, :]).astype(jnp.bfloat16)
        rows = jnp.dot(picks, table, preferred_element_type=jnp.float32).astype(jnp.bfloat16)
        rows = rows.reshape(owners, ROW_LIMIT, features)
        got = lax.all_to_all(rows, "table", split_axis=0, concat_axis=0, tiled=True)
        return got.reshape(-1, features)

    def placed(mixing, permute):
        return jnp.dot(mixing, permute, preferred_element_type=jnp.float32).astype(jnp.bfloat16)

    mixing_a = placed(combine_table(slots[0, 0], weights[0, 0], listed), permute_a)
    mixing_b = placed(combine_table(slots[0, 1], weights[0, 1], listed), permute_b)
    gate_value = gate_a[0].astype(jnp.float32)
    incoming = cotangent_a[0].astype(jnp.float32)
    logistic = jax.nn.sigmoid(gate_value)
    grad_memory = (incoming * gate_value * logistic).astype(jnp.bfloat16)
    grad_rows = lax.dot_general(
        mixing_a, grad_memory, (((0,), (0,)), ((), ())), preferred_element_type=jnp.float32
    ).astype(jnp.bfloat16)
    outgoing = grad_rows.reshape(owners, ROW_LIMIT, sections, part)
    outgoing = jnp.transpose(outgoing, (2, 0, 1, 3)).reshape(sections * owners, ROW_LIMIT, part)
    arrived = lax.all_to_all(
        outgoing, ("section", "table"), split_axis=0, concat_axis=0, tiled=True
    )
    fetched_a = serve(received[:, 0])
    fetched_b = serve(received[:, 1])
    match = (row_index[:, None] == asked_a[None, :]).astype(jnp.bfloat16)
    grad_table = jnp.dot(match, arrived.reshape(-1, part), preferred_element_type=jnp.float32)
    memory = jnp.dot(mixing_a, fetched_a, preferred_element_type=jnp.float32)
    grad_gate = (incoming * memory * logistic * (1.0 + gate_value * (1.0 - logistic))).astype(
        jnp.bfloat16
    )
    scores = lax.dot_general(
        grad_memory, fetched_a, (((1,), (1,)), ((), ())), preferred_element_type=jnp.float32
    )
    scores = lax.dot_general(
        scores, permute_a.astype(jnp.float32), (((1,), (1,)), ((), ())),
        precision=lax.Precision.HIGHEST, preferred_element_type=jnp.float32,
    )
    chosen = slots[0, 0][:, :, None] == jnp.arange(listed, dtype=jnp.int32)[None, None, :]
    grad_weights = jnp.sum(jnp.where(chosen, scores[:, None, :], 0.0), axis=2)
    memory = jnp.dot(mixing_b, fetched_b, preferred_element_type=jnp.float32)
    gate_value = gate_b[0].astype(jnp.float32)
    mixed_b = (gate_value * jax.nn.sigmoid(gate_value) * memory).astype(jnp.bfloat16)
    return (mixed_b[None], grad_gate[None], grad_weights[None], grad_table)


def solution(mesh):
    return jax.shard_map(
        local,
        mesh=mesh,
        in_specs=(
            P("section", "table", None),
            P("section", "table", None),
            P("section", "table", None),
            P("table", None),
            P("section", None, "table", None),
            P("section", None, "table", None),
            P("section", None, "table", None),
        ),
        out_specs=(
            P("section", "table", None),
            P("section", "table", None),
            P("section", "table", None),
            P("table", "section"),
        ),
        check_vma=False,
    )
```

time: 191 us -> 111 us (0.58)
  the two profiles are of different devices: /device:TPU:15 before, /device:TPU:0 now
where the time goes in v1:
time: 111 us; the launch traced here: 110 us
  waiting for transfers between devices  54.2 us (49%)
  blocking collectives  17.3 us (16%)
  starting transfers between devices  14.5 us (13%)
  matrix products  11.9 us (11%)
  other arithmetic  8.72 us (8%)
  local copies, waits for them, and re-layouts  2.61 us (2%)
    all_to_all x2, waiting for transfers between devices, serve(): got = lax.all_to_all(rows, 'table', split_axis=0, concat_axis=0, tiled=True)  36.2 us
    all_to_all x1, waiting for transfers between devices, local(): lax.all_to_all(outgoing, ('section', 'table'), split_axis=0, concat_axis=...  18.1 us
    all_to_all x1, blocking collectives, local(): lax.all_to_all(requests, 'table', split_axis=0, concat_axis=0, tiled=True)  15.5 us
    all_to_all x2, starting transfers between devices, serve(): got = lax.all_to_all(rows, 'table', split_axis=0, concat_axis=0, tiled=True)  9.5 us
    all_to_all x1, starting transfers between devices, local(): lax.all_to_all(outgoing, ('section', 'table'), split_axis=0, concat_axis=...  5.01 us
    reduce_sum x1, other arithmetic, local(): grad_weights = jnp.sum(jnp.where(chosen, scores[:, None, :], 0.0), axis=2)  4.67 us
    dot_general x2, matrix products, serve(): jnp.dot(picks, table, preferred_element_type=jnp.float32)  3 us
    reduce_sum x1, other arithmetic, combine_table(): jnp.sum(jnp.where(matches, weight_rows[:, :, None], jnp.zeros_like(weight...  2.79 us
  transfers between devices with their start and end apart: 3, of which 3 were waited for; matrix products, arithmetic and copies ran while one was open for 16% of the time, Pallas kernels for 0%

profile of v1, /device:TPU:0, one launch (start us, length us, event | category | flops | bytes accessed | tf_op | source)
XLA Modules:
  0.0 110.1 jit_solution(5559966028380791021)
XLA Ops:
  0.6 0.0 copy-start
  0.6 0.7 bitcast_subtract_fusion
  1.4 0.2 convert_reduce_fusion
  1.6 0.2 convert_reduce_fusion.1
  1.8 0.2 select_reduce_fusion.3
  1.9 0.1 stack_reshape.7
  2.0 0.1 stack_reshape.6
  2.1 15.5 %all_to_all.20 = s32[16,2,8]{2,1,0:T(2,128)S(1)} all-to-all(s32[16,2,8]{2,1,0:T(2,128)S(1)} %copy.14), channel_id=1, replica_groups=mesh['section'=2,'table'=16] {'table'}, dimensions={0} | all-to-all | bytes 2048 | tf_op jit(solution)/shard_map/all_to_all | solution.py:38
  17.7 0.1 eq.150
  17.7 0.0 copy-done
  17.8 1.5 %fusion.3 = bf16[16,8,4096]{2,1,0:T(8,128)(2,1)} fusion(bf16[64,4096]{1,0:T(8,128)(2,1)S(1)} %copy-done, s32[128]{0:T(128)S(1)} %eq.150), kind=kOutput, calls=%fused_computation.8 | convolution fusion | flops 67641344 | bytes 1573376 | tf_op jit(solution)/shard_map/dot_general | solution.py:44
  19.2 3.7 %all-to-all-start.2 = ((bf16[16,8,4096]{2,1,0:T(8,128)(2,1)}), bf16[16,8,4096]{2,1,0:T(8,128)(2,1)S(1)}, u32[]{:S(2)}, u32[]{:S(2)}) async-start(bf16[16,8,4096]{2,1,0:T(8,128)(2,1)} %fusion.3), calls=%async_computation.2 | async-start | bytes 2097152 | tf_op jit(solution)/shard_map/all_to_all | solution.py:46
  22.9 0.1 eq.142
  23.0 1.5 %fusion.2 = bf16[16,8,4096]{2,1,0:T(8,128)(2,1)} fusion(bf16[64,4096]{1,0:T(8,128)(2,1)S(1)} %copy-done, s32[128]{0:T(128)S(1)} %eq.142), kind=kOutput, calls=%fused_computation.7 | convolution fusion | flops 67641344 | bytes 1573376 | tf_op jit(solution)/shard_map/dot_general | solution.py:44
  24.5 0.0 copy-start.2
  24.5 0.0 copy-start.3
  24.5 0.0 copy-start.5
  24.5 21.6 %all-to-all-done.2 = bf16[16,8,4096]{2,1,0:T(8,128)(2,1)S(1)} async-done(((bf16[16,8,4096]{2,1,0:T(8,128)(2,1)}), bf16[16,8,4096]{2,1,0:T(8,128)(2,1)S(1)}, u32[]{:S(2)}, u32[]{:S(2)}) %all-to-all-start.2) | async-done | bytes 1048608 | tf_op jit(solution)/shard_map/all_to_all | solution.py:46
  46.1 5.8 %all-to-all-start.1 = ((bf16[16,8,4096]{2,1,0:T(8,128)(2,1)}), bf16[16,8,4096]{2,1,0:T(8,128)(2,1)S(1)}, u32[]{:S(2)}, u32[]{:S(2)}) async-start(bf16[16,8,4096]{2,1,0:T(8,128)(2,1)} %fusion.2), calls=%async_computation.1 | async-start | bytes 2097152 | tf_op jit(solution)/shard_map/all_to_all | solution.py:46
  51.9 0.0 copy-done.2
  52.0 0.0 copy-done.3
  52.0 0.0 copy-done.5
  52.0 0.0 copy-start.6
  52.0 1.6 %fusion.27 = f32[64,128]{1,0:T(8,128)S(1)} fusion(bf16[16,8,4096]{2,1,0:T(8,128)(2,1)S(1)} %all-to-all-done.2, bf16[1,64,4096]{2,1,0:T(8,128)(2,1)S(1)} %copy-done.5, bf16[1,64,4096]{2,1,0:T(8,128)(2,1)} %param.8), kind=kOutput, calls=%fused_computation.45 | convolution fusion | flops 69206016 | bytes 2129920 | tf_op jit(solution)/shard_map/dot_general | solution.py:74
  53.6 0.3 fusion.35
  53.9 4.7 %select_reduce_fusion = (f32[64,128]{1,0:T(8,128)}, bf16[64,128]{1,0:T(8,128)(2,1)S(1)}) fusion(f32[64,128]{1,0:T(8,128)S(1)} %fusion.35, s32[64,128]{1,0:T(8,128)S(1)} %get-tuple-element.14, f32[64,128]{1,0:T(8,128)S(1)} %get-tuple-element.12), kind=kLoop, calls=%fused_computation.13 | loop fusion | flops 5226496 | bytes 147456 | tf_op jit(solution)/shard_map/reduce_sum | solution.py:82
  58.5 0.2 convolution_convert_fusion.3
  58.7 0.0 copy-done.6
  58.7 0.5 convolution_convert_fusion
  59.3 1.1 copy.15
  60.3 14.6 %all-to-all-done.1 = bf16[16,8,4096]{2,1,0:T(8,128)(2,1)S(1)} async-done(((bf16[16,8,4096]{2,1,0:T(8,128)(2,1)}), bf16[16,8,4096]{2,1,0:T(8,128)(2,1)S(1)}, u32[]{:S(2)}, u32[]{:S(2)}) %all-to-all-start.1) | async-done | bytes 1048608 | tf_op jit(solution)/shard_map/all_to_all | solution.py:46
  74.9 0.0 copy-start.1
  74.9 0.0 copy-start.4
  74.9 1.0 copy-done.1
  75.9 5.0 %all-to-all-start.3 = ((bf16[32,8,2048]{2,1,0:T(8,128)(2,1)}), bf16[32,8,2048]{2,1,0:T(8,128)(2,1)S(1)}, u32[]{:S(2)}, u32[]{:S(2)}) async-start(bf16[32,8,2048]{2,1,0:T(8,128)(2,1)} %bitcast.21), calls=%async_computation.3 | async-start | bytes 2097152 | tf_op jit(solution)/shard_map/all_to_all | solution.py:63
  81.0 2.8 %select_reduce_fusion.2 = bf16[64,128]{1,0:T(8,128)(2,1)S(1)} fusion(f32[64,128]{1,0:T(8,128)S(1)} %get-tuple-element.13, s32[64,128]{1,0:T(8,128)S(1)} %get-tuple-element.15), kind=kLoop, calls=%fused_computation.16 | loop fusion | flops 3137536 | bytes 81920 | tf_op jit(solution)/shard_map/reduce_sum | solution.py:24
  83.7 0.1 reshape.220
  83.8 1.8 %all-gather = s32[2,1,128]{2,1,0:T(1,128)S(1)} all-gather(s32[1,1,128]{2,1,0:T(1,128)S(1)} %reshape.220), channel_id=1, replica_groups=mesh['section'=2,'table'=16] {'section'}, dimensions={0}, use_global_device_ids=true | all-gather | bytes 1536 | tf_op jit(solution)/shard_map/all_gather | solution.py:39
  85.6 0.0 copy-done.4
  85.6 2.7 %fusion.6 = bf16[1,64,4096]{2,1,0:T(8,128)(2,1)} fusion(bf16[16,8,4096]{2,1,0:T(8,128)(2,1)} %copy-done.1, bf16[1,64,4096]{2,1,0:T(8,128)(2,1)S(1)} %copy-done.4, s32[128]{0:T(128)S(1)} %multiply_add_fusion.1, bf16[64,128]{1,0:T(8,128)(2,1)S(1)} %select_reduce_fusion.2), kind=kOutput, calls=%fused_computation.11 | convolution fusion | flops 71065600 | bytes 2114048 | tf_op jit(solution)/shard_map/dot_general | solution.py:83
  88.3 2.6 %fusion.7 = bf16[1,64,4096]{2,1,0:T(8,128)(2,1)} fusion(bf16[64,128]{1,0:T(8,128)(2,1)S(1)} %convolution_convert_fusion.3, bf16[1,64,4096]{2,1,0:T(8,128)(2,1)} %param.8, bf16[1,64,4096]{2,1,0:T(8,128)(2,1)} %param.7, bf16[16,8,4096]{2,1,0:T(8,128)(2,1)S(1)} %all-to-all-done.2), kind=kOutput, calls=%fused_computation.12 | convolution fusion | flops 70254592 | bytes 2637824 | tf_op jit(solution)/shard_map/dot_general | solution.py:70
  90.9 18.1 %all-to-all-done.3 = bf16[32,8,2048]{2,1,0:T(8,128)(2,1)S(1)} async-done(((bf16[32,8,2048]{2,1,0:T(8,128)(2,1)}), bf16[32,8,2048]{2,1,0:T(8,128)(2,1)S(1)}, u32[]{:S(2)}, u32[]{:S(2)}) %all-to-all-start.3) | async-done | bytes 1048608 | tf_op jit(solution)/shard_map/all_to_all | solution.py:63
  109.0 1.1 fusion.25
  (7 shorter events, 0.1 us)
Async XLA Ops:
  0.6 17.1 %copy-start = (bf16[64,4096]{1,0:T(8,128)(2,1)S(1)}, bf16[64,4096]{1,0:T(8,128)(2,1)}, u32[]{:S(2)}) copy-start(bf16[64,4096]{1,0:T(8,128)(2,1)} %param.10) | copy-start | bytes 1572868
  19.2 26.9 %all-to-all-start.2 = ((bf16[16,8,4096]{2,1,0:T(8,128)(2,1)}), bf16[16,8,4096]{2,1,0:T(8,128)(2,1)S(1)}, u32[]{:S(2)}, u32[]{:S(2)}) async-start(bf16[16,8,4096]{2,1,0:T(8,128)(2,1)} %fusion.3), calls=%async_computation.2 | async-start | bytes 2097152 | tf_op jit(solution)/shard_map/all_to_all | solution.py:46
  24.5 27.4 %copy-start.2 = (s32[1,2,64,128]{3,2,1,0:T(8,128)S(1)}, s32[1,2,64,128]{3,2,1,0:T(8,128)}, u32[]{:S(2)}) copy-start(s32[1,2,64,128]{3,2,1,0:T(8,128)} %param.12) | copy-start | bytes 196612
  24.5 27.5 %copy-start.3 = (f32[1,2,64,128]{3,2,1,0:T(8,128)S(1)}, f32[1,2,64,128]{3,2,1,0:T(8,128)}, u32[]{:S(2)}) copy-start(f32[1,2,64,128]{3,2,1,0:T(8,128)} %param.13) | copy-start | bytes 196612
  24.5 27.5 %copy-start.5 = (bf16[1,64,4096]{2,1,0:T(8,128)(2,1)S(1)}, bf16[1,64,4096]{2,1,0:T(8,128)(2,1)}, u32[]{:S(2)}) copy-start(bf16[1,64,4096]{2,1,0:T(8,128)(2,1)} %param.7) | copy-start | bytes 1572868
  46.1 28.8 %all-to-all-start.1 = ((bf16[16,8,4096]{2,1,0:T(8,128)(2,1)}), bf16[16,8,4096]{2,1,0:T(8,128)(2,1)S(1)}, u32[]{:S(2)}, u32[]{:S(2)}) async-start(bf16[16,8,4096]{2,1,0:T(8,128)(2,1)} %fusion.2), calls=%async_computation.1 | async-start | bytes 2097152 | tf_op jit(solution)/shard_map/all_to_all | solution.py:46
  52.0 6.8 %copy-start.6 = (bf16[1,64,4096]{2,1,0:T(8,128)(2,1)S(1)}, bf16[1,64,4096]{2,1,0:T(8,128)(2,1)}, u32[]{:S(2)}) copy-start(bf16[1,64,4096]{2,1,0:T(8,128)(2,1)} %param.8) | copy-start | bytes 1572868
  74.9 1.0 copy-start.1
  74.9 10.7 %copy-start.4 = (bf16[1,64,4096]{2,1,0:T(8,128)(2,1)S(1)}, bf16[1,64,4096]{2,1,0:T(8,128)(2,1)}, u32[]{:S(2)}) copy-start(bf16[1,64,4096]{2,1,0:T(8,128)(2,1)} %param.9) | copy-start | bytes 1572868
  75.9 33.1 %all-to-all-start.3 = ((bf16[32,8,2048]{2,1,0:T(8,128)(2,1)}), bf16[32,8,2048]{2,1,0:T(8,128)(2,1)S(1)}, u32[]{:S(2)}, u32[]{:S(2)}) async-start(bf16[32,8,2048]{2,1,0:T(8,128)(2,1)} %bitcast.21), calls=%async_computation.3 | async-start | bytes 2097152 | tf_op jit(solution)/shard_map/all_to_all | solution.py:63

commit v2 on v1

v2 whole, which is shorter than its diff:
```python
import jax
import jax.numpy as jnp
from jax import lax
from jax.experimental import pallas as pl
from jax.experimental.pallas import tpu as pltpu
from jax.sharding import PartitionSpec as P

ROW_LIMIT = 8
CHUNK = 512
MESH = pl.DeviceIdType.MESH


def place_rows(row_list, rows_dev, owners, capacity):
    owner_of = row_list // rows_dev
    offset = row_list - owner_of * rows_dev
    listed = row_list.shape[0]
    same = owner_of[:, None] == owner_of[None, :]
    before = jnp.arange(listed)[None, :] < jnp.arange(listed)[:, None]
    position = jnp.sum((same & before).astype(jnp.int32), axis=1)
    place = owner_of * capacity + position
    permute = (place[:, None] == jnp.arange(owners * capacity, dtype=jnp.int32)[None, :])
    requests = jnp.max(jnp.where(permute, offset[:, None], -1), axis=0)
    return requests.reshape(owners, capacity), permute.astype(jnp.bfloat16)


def combine_table(slot_rows, weight_rows, listed):
    matches = slot_rows[:, :, None] == jnp.arange(listed, dtype=jnp.int32)[None, None, :]
    return jnp.sum(
        jnp.where(matches, weight_rows[:, :, None], jnp.zeros_like(weight_rows[:, :, None])), axis=1
    ).astype(jnp.bfloat16)


def drain(block, sem):
    pltpu.make_async_copy(block, block, sem).wait()


def exchange(
    gate_a, cot_a, gate_b, table, asks, mix_a, mix_b, permute, slots,
    mixed_b, grad_gate, grad_weights, grad_table,
    asked, rows_out, fetched, grads_out, arrived, grad_memory, scores,
    ask_send, ask_recv, grad_send, grad_recv, row_send, row_recv,
):
    sections = lax.axis_size("section")
    owners = lax.axis_size("table")
    sec = lax.axis_index("section")
    me = lax.axis_index("table")
    rows_dev, features = table.shape
    part = features // sections
    everyone = sections * owners
    mine = sec * owners + me
    f32 = jnp.float32

    def peers(step, first):
        @pl.loop(first, everyone)
        def _(hop):
            over = lax.rem(mine + hop, everyone)
            step(over // owners, lax.rem(over, owners))

    barrier = pltpu.get_barrier_semaphore()
    peers(
        lambda s, t: pl.semaphore_signal(
            barrier, inc=1, device_id={"section": s, "table": t}, device_id_type=MESH
        ),
        1,
    )

    @pl.loop(0, features // CHUNK)
    def _(c):
        cols = pl.ds(pl.multiple_of(c * CHUNK, CHUNK), CHUNK)
        gate = gate_a[:, cols].astype(f32)
        value = (cot_a[:, cols].astype(f32) * gate * jax.nn.sigmoid(gate)).astype(jnp.bfloat16)
        grad_memory[:, cols] = value
        rows = lax.dot_general(
            mix_a[...], value, (((0,), (0,)), ((), ())), preferred_element_type=f32
        ).reshape(owners, 2, ROW_LIMIT, CHUNK)[:, 0]
        per = part // CHUNK
        inner = pl.ds(pl.multiple_of(lax.rem(c, per) * CHUNK, CHUNK), CHUNK)
        grads_out[c // per, :, :, inner] = rows.astype(jnp.bfloat16)

    pl.semaphore_wait(barrier, everyone - 1)

    def remote(source, target, send, recv, s, t):
        pltpu.make_async_remote_copy(
            src_ref=source, dst_ref=target, send_sem=send, recv_sem=recv,
            device_id={"section": s, "table": t}, device_id_type=MESH,
        ).start()

    peers(lambda s, t: remote(asks.at[t], asked.at[mine], ask_send, ask_recv, s, t), 1)
    pltpu.make_async_copy(asks.at[me], asked.at[mine], ask_recv).start()
    peers(
        lambda s, t: remote(grads_out.at[s, t], arrived.at[mine], grad_send, grad_recv, s, t), 1
    )
    pltpu.make_async_copy(grads_out.at[sec, me], arrived.at[mine], grad_recv).start()

    drain(asked, ask_recv)
    wanted = asked[pl.ds(sec * owners, owners)].reshape(owners * 2 * ROW_LIMIT, -1)[:, :rows_dev]

    @pl.loop(0, features // CHUNK)
    def _(c):
        cols = pl.ds(pl.multiple_of(c * CHUNK, CHUNK), CHUNK)
        rows = jnp.dot(wanted, table[:, cols], preferred_element_type=f32).astype(jnp.bfloat16)
        rows_out[:, :, cols] = rows.reshape(owners, 2 * ROW_LIMIT, CHUNK)

    @pl.loop(1, owners)
    def _(hop):
        t = lax.rem(me + hop, owners)
        remote(rows_out.at[t], fetched.at[me], row_send, row_recv, sec, t)

    pltpu.make_async_copy(rows_out.at[me], fetched.at[me], row_recv).start()

    asked_a = asked[...].astype(f32)[:, :ROW_LIMIT].reshape(everyone * ROW_LIMIT, -1)
    asked_a = asked_a.astype(jnp.bfloat16)
    drain(arrived, grad_recv)

    @pl.loop(0, part // CHUNK)
    def _(c):
        cols = pl.ds(pl.multiple_of(c * CHUNK, CHUNK), CHUNK)
        block = arrived[:, :, cols].reshape(everyone * ROW_LIMIT, CHUNK)
        total = lax.dot_general(
            asked_a, block, (((0,), (0,)), ((), ())), preferred_element_type=f32
        )
        grad_table[:, cols] = total[:rows_dev]

    drain(fetched, row_recv)
    scores[...] = jnp.zeros_like(scores)

    @pl.loop(0, features // CHUNK)
    def _(c):
        cols = pl.ds(pl.multiple_of(c * CHUNK, CHUNK), CHUNK)
        rows = fetched[:, :, cols].reshape(owners * 2 * ROW_LIMIT, CHUNK)
        memory = jnp.dot(mix_a[...], rows, preferred_element_type=f32)
        gate = gate_a[:, cols].astype(f32)
        sig = jax.nn.sigmoid(gate)
        incoming = cot_a[:, cols].astype(f32)
        grad_gate[:, cols] = (incoming * memory * sig * (1.0 + gate * (1.0 - sig))).astype(
            jnp.bfloat16
        )
        scores[...] += lax.dot_general(
            grad_memory[:, cols], rows, (((1,), (1,)), ((), ())), preferred_element_type=f32
        )
        memory = jnp.dot(mix_b[...], rows, preferred_element_type=f32)
        gate = gate_b[:, cols].astype(f32)
        mixed_b[:, cols] = (gate * jax.nn.sigmoid(gate) * memory).astype(jnp.bfloat16)

    listed = lax.dot_general(
        scores[...], permute[...], (((1,), (1,)), ((), ())),
        precision=lax.Precision.HIGHEST, preferred_element_type=f32,
    )
    grad_weights[...] = jnp.take_along_axis(listed, slots[...], axis=1)
    drain(asked.at[pl.ds(0, everyone - 1)], ask_send)
    drain(arrived.at[pl.ds(0, everyone - 1)], grad_send)
    drain(rows_out.at[pl.ds(0, owners - 1)], row_send)


def local(gate_a, cotangent_a, gate_b, table, row_ids, slots, weights):
    owners = lax.axis_size("table")
    sections = lax.axis_size("section")
    rows_dev, features = table.shape
    tokens = gate_a.shape[1]
    listed = row_ids.shape[-1]
    part = features // sections
    lanes = -(-rows_dev // 128) * 128
    requests_a, permute_a = place_rows(row_ids[0, 0, 0], rows_dev, owners, ROW_LIMIT)
    requests_b, permute_b = place_rows(row_ids[0, 1, 0], rows_dev, owners, ROW_LIMIT)
    requests = jnp.concatenate([requests_a, requests_b], axis=1)
    asks = (requests[:, :, None] == jnp.arange(lanes, dtype=jnp.int32)).astype(jnp.bfloat16)

    def widen(permute, which):
        split = permute.reshape(listed, owners, ROW_LIMIT)
        pair = [jnp.zeros_like(split), jnp.zeros_like(split)]
        pair[which] = split
        return jnp.concatenate(pair, axis=2).reshape(listed, owners * 2 * ROW_LIMIT)

    def placed(mixing, permute):
        return jnp.dot(mixing, permute, preferred_element_type=jnp.float32).astype(jnp.bfloat16)

    wide_a, wide_b = widen(permute_a, 0), widen(permute_b, 1)
    mix_a = placed(combine_table(slots[0, 0], weights[0, 0], listed), wide_a)
    mix_b = placed(combine_table(slots[0, 1], weights[0, 1], listed), wide_b)
    bf16 = jnp.bfloat16
    everyone = sections * owners
    vmem = pl.BlockSpec(memory_space=pltpu.VMEM)
    mixed_b, grad_gate, grad_weights, grad_table = pl.pallas_call(
        exchange,
        out_shape=(
            jax.ShapeDtypeStruct((tokens, features), bf16),
            jax.ShapeDtypeStruct((tokens, features), bf16),
            jax.ShapeDtypeStruct((tokens, listed), jnp.float32),
            jax.ShapeDtypeStruct((rows_dev, part), jnp.float32),
        ),
        in_specs=[vmem] * 9,
        out_specs=(vmem,) * 4,
        scratch_shapes=[
            pltpu.VMEM((everyone, 2 * ROW_LIMIT, lanes), bf16),
            pltpu.VMEM((owners, 2 * ROW_LIMIT, features), bf16),
            pltpu.VMEM((owners, 2 * ROW_LIMIT, features), bf16),
            pltpu.VMEM((sections, owners, ROW_LIMIT, part), bf16),
            pltpu.VMEM((everyone, ROW_LIMIT, part), bf16),
            pltpu.VMEM((tokens, features), bf16),
            pltpu.VMEM((tokens, owners * 2 * ROW_LIMIT), jnp.float32),
        ]
        + [pltpu.SemaphoreType.DMA] * 6,
        compiler_params=pltpu.CompilerParams(
            collective_id=0, has_side_effects=True, vmem_limit_bytes=60 * 1024 * 1024
        ),
    )(
        gate_a[0], cotangent_a[0], gate_b[0], table, asks, mix_a, mix_b,
        wide_a.astype(jnp.float32), slots[0, 0],
    )
    return mixed_b[None], grad_gate[None], grad_weights[None], grad_table


def solution(mesh):
    return jax.shard_map(
        local,
        mesh=mesh,
        in_specs=(
            P("section", "table", None),
            P("section", "table", None),
            P("section", "table", None),
            P("table", None),
            P("section", None, "table", None),
            P("section", None, "table", None),
            P("section", None, "table", None),
        ),
        out_specs=(
            P("section", "table", None),
            P("section", "table", None),
            P("section", "table", None),
            P("table", "section"),
        ),
        check_vma=False,
    )
```

time: 111 us -> 101 us (0.910)
  the two profiles are of different devices: /device:TPU:0 before, /device:TPU:15 now
where the time goes in v2:
time: 101 us
  Pallas kernels  84.5 us (84%)
  other arithmetic  8.58 us (8%)
  local copies, waits for them, and re-layouts  5.24 us (5%)
  matrix products  1.55 us (2%)
    pallas_call x1, Pallas kernels, local(): pl.pallas_call(exchange, out_shape=(jax.ShapeDtypeStruct((tokens, feature...  84.5 us
    reduce_sum x1, other arithmetic, combine_table(): jnp.sum(jnp.where(matches, weight_rows[:, :, None], jnp.zeros_like(weight...  5.76 us
    unnamed x14, local copies, waits for them, and re-layouts  4.15 us

profile of v2, /device:TPU:15, one launch (start us, length us, event | category | flops | bytes accessed | tf_op | source)
XLA Modules:
  0.0 100.6 jit_solution(11444937742098336544)
XLA Ops:
  0.6 0.0 copy-start.3
  0.6 0.7 bitcast_subtract_fusion.1
  1.4 0.2 convert_reduce_fusion.1
  1.5 0.2 convert_reduce_fusion
  1.7 0.2 select_reduce_fusion.2
  1.9 0.1 reshape.222
  2.0 0.1 reshape.221
  2.1 0.1 pad_add_fusion
  2.1 0.1 broadcast_compare_fusion
  2.3 0.1 copy.12
  2.4 0.7 fusion.asks
  3.2 0.8 slice_bitcast_fusion.1
  3.9 0.0 copy-start.2
  3.9 0.0 copy-done.3
  4.0 5.8 %select_reduce_fusion = (bf16[64,128]{1,0:T(8,128)(2,1)S(1)}, bf16[64,128]{1,0:T(8,128)(2,1)S(1)}) fusion(f32[64,128]{1,0:T(8,128)S(1)} %get-tuple-element.18, s32[64,128]{1,0:T(8,128)S(1)} %get-tuple-element.16, f32[64,128]{1,0:T(8,128)S(1)} %get-tuple-element.19, s32[64,128]{1,0:T(8,128)S(1)} %get-tuple-element.17.slots), kind=kLoop, calls=%fused_computation | loop fusion | flops 6275072 | bytes 163840 | tf_op jit(solution)/shard_map/reduce_sum | solution.py:28
  9.7 0.8 convolution_convert_fusion.mix_b
  10.5 0.8 convolution_convert_fusion.1.mix_a
  11.3 0.7 convert_convert_fusion.permute
  11.9 0.0 copy-done.2
  11.9 84.5 %shard_map.102 = (bf16[64,4096]{1,0:T(8,128)(2,1)}, bf16[64,4096]{1,0:T(8,128)(2,1)}, f32[64,128]{1,0:T(8,128)}, f32[64,2048]{1,0:T(8,128)}) custom-call(bf16[64,4096]{1,0:T(8,128)(2,1)} %bitcast.42, bf16[64,4096]{1,0:T(8,128)(2,1)} %bitcast.43, bf16[64,4096]{1,0:T(8,128)(2,1)} %bitcast.44, bf16[64,4096]{1,0:T(8,128)(2,1)} %table.1, ...), custom_call_target="tpu_custom_call" | custom-call | tf_op jit(solution)/shard_map/pallas_call | solution.py:183
  96.4 0.0 copy-start.1
  96.4 1.9 %copy.17 = bf16[1,64,4096]{2,1,0:T(8,128)(2,1)} copy(bf16[1,64,4096]{2,1,0:T(8,128)(2,1)} %bitcast.41) | data formatting | bytes 1048576
  98.4 0.0 copy-done.1
  98.4 0.0 copy-start.4
  98.4 0.0 copy-start
  98.4 0.8 copy.18
  99.2 0.0 copy-done.4
  99.2 0.6 copy.19
  99.8 0.0 copy-done
  99.8 0.8 copy.20
  (6 shorter events, 0.0 us)
Async XLA Ops:
  0.6 3.3 %copy-start.3 = (f32[1,2,64,128]{3,2,1,0:T(8,128)S(1)}, f32[1,2,64,128]{3,2,1,0:T(8,128)}, u32[]{:S(2)}) copy-start(f32[1,2,64,128]{3,2,1,0:T(8,128)} %param.13) | copy-start | bytes 196612
  3.9 8.0 %copy-start.2 = (s32[64,128]{1,0:T(8,128)}, s32[64,128]{1,0:T(8,128)S(1)}, u32[]{:S(2)}) copy-start(s32[64,128]{1,0:T(8,128)S(1)} %get-tuple-element.17.slots) | copy-start | bytes 98308
  96.4 1.9 %copy-start.1 = (bf16[64,4096]{1,0:T(8,128)(2,1)S(1)}, bf16[64,4096]{1,0:T(8,128)(2,1)}, u32[]{:S(2)}) copy-start(bf16[64,4096]{1,0:T(8,128)(2,1)} %get-tuple-element.9) | copy-start | bytes 1572868
  98.4 0.8 copy-start.4
  98.4 1.4 %copy-start = (f32[64,2048]{1,0:T(8,128)S(1)}, f32[64,2048]{1,0:T(8,128)}, u32[]{:S(2)}) copy-start(f32[64,2048]{1,0:T(8,128)} %get-tuple-element.35) | copy-start | bytes 1572868

commit v3 on v2

--- a/solution.py
+++ b/solution.py
@@ -7,26 +7,53 @@
 
 ROW_LIMIT = 8
 CHUNK = 512
+GROUP = 8
 MESH = pl.DeviceIdType.MESH
 
 
-def place_rows(row_list, rows_dev, owners, capacity):
-    owner_of = row_list // rows_dev
-    offset = row_list - owner_of * rows_dev
-    listed = row_list.shape[0]
-    same = owner_of[:, None] == owner_of[None, :]
-    before = jnp.arange(listed)[None, :] < jnp.arange(listed)[:, None]
-    position = jnp.sum((same & before).astype(jnp.int32), axis=1)
-    place = owner_of * capacity + position
-    permute = (place[:, None] == jnp.arange(owners * capacity, dtype=jnp.int32)[None, :])
-    requests = jnp.max(jnp.where(permute, offset[:, None], -1), axis=0)
-    return requests.reshape(owners, capacity), permute.astype(jnp.bfloat16)
-
-
-def combine_table(slot_rows, weight_rows, listed):
-    matches = slot_rows[:, :, None] == jnp.arange(listed, dtype=jnp.int32)[None, None, :]
-    return jnp.sum(
-        jnp.where(matches, weight_rows[:, :, None], jnp.zeros_like(weight_rows[:, :, None])), axis=1
+def mix_picks(slot_rows, weight_rows):
+    picks = slot_rows.shape[1]
+    lane = lax.broadcasted_iota(jnp.int32, slot_rows.shape, 1)
+
+    def group(_, carry):
+        slot, weight, total = carry
+        for p in range(GROUP):
+            hit = slot[:, p : p + 1] == lane
+            total = total + jnp.where(hit, weight[:, p : p + 1], 0.0)
+        return (
+            pltpu.roll(slot, picks - GROUP, 1), pltpu.roll(weight, picks - GROUP, 1), total
+        )
+
+    start = (slot_rows, weight_rows, jnp.zeros(weight_rows.shape, jnp.float32))
+    return lax.fori_loop(0, picks // GROUP, group, start)[2].astype(jnp.bfloat16)
+
+
+def place_rows(ids, owners, rows_dev, lanes, base):
+    listed = ids.shape[1]
+    f32, bf16 = jnp.float32, jnp.bfloat16
+    owner = lax.broadcasted_iota(jnp.int32, (owners, listed), 0)
+    first = owner * rows_dev
+    member = ((ids >= first) & (ids < first + rows_dev)).astype(f32)
+    before = lax.broadcasted_iota(jnp.int32, (listed, listed), 0) < lax.broadcasted_iota(
+        jnp.int32, (listed, listed), 1
+    )
+    earlier = jnp.dot(
+        member.astype(bf16), before.astype(f32).astype(bf16), preferred_element_type=f32
+    )
+    spot = earlier + (owner * (2 * ROW_LIMIT) + base).astype(f32)
+    place = jnp.sum(member * spot, axis=0, keepdims=True).astype(jnp.int32)
+    offset = ids - jnp.sum(member * first.astype(f32), axis=0, keepdims=True).astype(jnp.int32)
+    space = lax.broadcasted_iota(jnp.int32, (owners * 2 * ROW_LIMIT, listed), 0)
+    wide = (space == place).astype(f32).astype(bf16)
+    row = lax.broadcasted_iota(jnp.int32, (lanes, listed), 0)
+    held = (row == offset).astype(f32).astype(bf16)
+    ask = lax.dot_general(wide, held, (((1,), (1,)), ((), ())), preferred_element_type=f32)
+    return wide, ask
+
+
+def spread(mixing, wide):
+    return lax.dot_general(
+        mixing, wide, (((1,), (1,)), ((), ())), preferred_element_type=jnp.float32
     ).astype(jnp.bfloat16)
 
 
@@ -35,9 +62,9 @@
 
 
 def exchange(
-    gate_a, cot_a, gate_b, table, asks, mix_a, mix_b, permute, slots,
+    gate_a, cot_a, gate_b, table, row_ids, slots, weights,
     mixed_b, grad_gate, grad_weights, grad_table,
-    asked, rows_out, fetched, grads_out, arrived, grad_memory, scores,
+    asks, mix_a, asked, rows_out, fetched, grads_out, arrived, grad_memory, scores,
     ask_send, ask_recv, grad_send, grad_recv, row_send, row_recv,
 ):
     sections = lax.axis_size("section")
@@ -64,6 +91,23 @@
         1,
     )
 
+    lanes = asks.shape[-1]
+    ids = row_ids[...]
+    wide_a, ask_a = place_rows(ids[0:1], owners, rows_dev, lanes, 0)
+    wide_b, ask_b = place_rows(ids[1:2], owners, rows_dev, lanes, ROW_LIMIT)
+    asks[...] = (ask_a + ask_b).astype(jnp.bfloat16).reshape(asks.shape)
+    pl.semaphore_wait(barrier, everyone - 1)
+
+    def remote(source, target, send, recv, s, t):
+        pltpu.make_async_remote_copy(
+            src_ref=source, dst_ref=target, send_sem=send, recv_sem=recv,
+            device_id={"section": s, "table": t}, device_id_type=MESH,
+        ).start()
+
+    peers(lambda s, t: remote(asks.at[t], asked.at[mine], ask_send, ask_recv, s, t), 1)
+    pltpu.make_async_copy(asks.at[me], asked.at[mine], ask_recv).start()
+    mix_a[...] = spread(mix_picks(slots[0], weights[0]), wide_a)
+
     @pl.loop(0, features // CHUNK)
     def _(c):
         cols = pl.ds(pl.multiple_of(c * CHUNK, CHUNK), CHUNK)
@@ -77,16 +121,6 @@
         inner = pl.ds(pl.multiple_of(lax.rem(c, per) * CHUNK, CHUNK), CHUNK)
         grads_out[c // per, :, :, inner] = rows.astype(jnp.bfloat16)
 
-    pl.semaphore_wait(barrier, everyone - 1)
-
-    def remote(source, target, send, recv, s, t):
-        pltpu.make_async_remote_copy(
-            src_ref=source, dst_ref=target, send_sem=send, recv_sem=recv,
-            device_id={"section": s, "table": t}, device_id_type=MESH,
-        ).start()
-
-    peers(lambda s, t: remote(asks.at[t], asked.at[mine], ask_send, ask_recv, s, t), 1)
-    pltpu.make_async_copy(asks.at[me], asked.at[mine], ask_recv).start()
     peers(
         lambda s, t: remote(grads_out.at[s, t], arrived.at[mine], grad_send, grad_recv, s, t), 1
     )
@@ -108,6 +142,7 @@
 
     pltpu.make_async_copy(rows_out.at[me], fetched.at[me], row_recv).start()
 
+    mix_b = spread(mix_picks(slots[1], weights[1]), wide_b)
     asked_a = asked[...].astype(f32)[:, :ROW_LIMIT].reshape(everyone * ROW_LIMIT, -1)
     asked_a = asked_a.astype(jnp.bfloat16)
     drain(arrived, grad_recv)
@@ -138,15 +173,15 @@
         scores[...] += lax.dot_general(
             grad_memory[:, cols], rows, (((1,), (1,)), ((), ())), preferred_element_type=f32
         )
-        memory = jnp.dot(mix_b[...], rows, preferred_element_type=f32)
+        memory = jnp.dot(mix_b, rows, preferred_element_type=f32)
         gate = gate_b[:, cols].astype(f32)
         mixed_b[:, cols] = (gate * jax.nn.sigmoid(gate) * memory).astype(jnp.bfloat16)
 
     listed = lax.dot_general(
-        scores[...], permute[...], (((1,), (1,)), ((), ())),
+        scores[...], wide_a.astype(f32), (((1,), (0,)), ((), ())),
         precision=lax.Precision.HIGHEST, preferred_element_type=f32,
     )
-    grad_weights[...] = jnp.take_along_axis(listed, slots[...], axis=1)
+    grad_weights[...] = jnp.take_along_axis(listed, slots[0], axis=1)
     drain(asked.at[pl.ds(0, everyone - 1)], ask_send)
     drain(arrived.at[pl.ds(0, everyone - 1)], grad_send)
     drain(rows_out.at[pl.ds(0, owners - 1)], row_send)
@@ -160,23 +195,6 @@
     listed = row_ids.shape[-1]
     part = features // sections
     lanes = -(-rows_dev // 128) * 128
-    requests_a, permute_a = place_rows(row_ids[0, 0, 0], rows_dev, owners, ROW_LIMIT)
-    requests_b, permute_b = place_rows(row_ids[0, 1, 0], rows_dev, owners, ROW_LIMIT)
-    requests = jnp.concatenate([requests_a, requests_b], axis=1)
-    asks = (requests[:, :, None] == jnp.arange(lanes, dtype=jnp.int32)).astype(jnp.bfloat16)
-
-    def widen(permute, which):
-        split = permute.reshape(listed, owners, ROW_LIMIT)
-        pair = [jnp.zeros_like(split), jnp.zeros_like(split)]
-        pair[which] = split
-        return jnp.concatenate(pair, axis=2).reshape(listed, owners * 2 * ROW_LIMIT)
-
-    def placed(mixing, permute):
-        return jnp.dot(mixing, permute, preferred_element_type=jnp.float32).astype(jnp.bfloat16)
-
-    wide_a, wide_b = widen(permute_a, 0), widen(permute_b, 1)
-    mix_a = placed(combine_table(slots[0, 0], weights[0, 0], listed), wide_a)
-    mix_b = placed(combine_table(slots[0, 1], weights[0, 1], listed), wide_b)
     bf16 = jnp.bfloat16
     everyone = sections * owners
     vmem = pl.BlockSpec(memory_space=pltpu.VMEM)
@@ -188,9 +206,11 @@
             jax.ShapeDtypeStruct((tokens, listed), jnp.float32),
             jax.ShapeDtypeStruct((rows_dev, part), jnp.float32),
         ),
-        in_specs=[vmem] * 9,
+        in_specs=[vmem] * 7,
         out_specs=(vmem,) * 4,
         scratch_shapes=[
+            pltpu.VMEM((owners, 2 * ROW_LIMIT, lanes), bf16),
+            pltpu.VMEM((tokens, owners * 2 * ROW_LIMIT), bf16),
             pltpu.VMEM((everyone, 2 * ROW_LIMIT, lanes), bf16),
             pltpu.VMEM((owners, 2 * ROW_LIMIT, features), bf16),
             pltpu.VMEM((owners, 2 * ROW_LIMIT, features), bf16),
@@ -204,8 +224,7 @@
             collective_id=0, has_side_effects=True, vmem_limit_bytes=60 * 1024 * 1024
         ),
     )(
-        gate_a[0], cotangent_a[0], gate_b[0], table, asks, mix_a, mix_b,
-        wide_a.astype(jnp.float32), slots[0, 0],
+        gate_a[0], cotangent_a[0], gate_b[0], table, row_ids[0, :, 0], slots[0], weights[0]
     )
     return mixed_b[None], grad_gate[None], grad_weights[None], grad_table
 

time: 101 us -> 93.8 us (0.929)
  other arithmetic: 8.58 us -> 0 us
  Pallas kernels: 84.5 us -> 88.8 us
  matrix products: 1.55 us -> 0 us
  local copies, waits for them, and re-layouts: 5.24 us -> 4.14 us
    reduce_sum x3 -> x0, other arithmetic: 6.1 us -> none  [the longest x1 5.76 us: combine_table(): jnp.sum(jnp.where(matches, weight_rows[:, :, None], jnp.zeros_like(weight...]
    pallas_call x1, Pallas kernels: 84.5 us -> 88.8 us  [local(): pl.pallas_call(exchange, out_shape=(jax.ShapeDtypeStruct((tokens, feature...]
    dot_general x2 -> x0, matrix products: 1.55 us -> none  [placed(): jnp.dot(mixing, permute, preferred_element_type=jnp.float32)]
    convert_element_type x2 -> x0, other arithmetic: 1.4 us -> none  [the longest x1 0.73 us: local(): (requests[:, :, None] == jnp.arange(lanes, dtype=jnp.int32)).astype(jnp.b...]
    unnamed x14 -> x10, local copies, waits for them, and re-layouts: 4.15 us -> 4.14 us
where the time goes in v3:
time: 93.8 us; the launch traced here: 93.6 us
  Pallas kernels  88.8 us (95%)
  local copies, waits for them, and re-layouts  4.14 us (4%)
    pallas_call x1, Pallas kernels, local(): pl.pallas_call(exchange, out_shape=(jax.ShapeDtypeStruct((tokens, feature...  88.8 us
    unnamed x10, local copies, waits for them, and re-layouts  4.14 us

profile of v3, /device:TPU:15, one launch (start us, length us, event | category | flops | bytes accessed | tf_op | source)
XLA Modules:
  0.0 93.6 jit_solution(9436373022668050256)
XLA Ops:
  0.6 88.8 %shard_map.102 = (bf16[64,4096]{1,0:T(8,128)(2,1)}, bf16[64,4096]{1,0:T(8,128)(2,1)}, f32[64,128]{1,0:T(8,128)}, f32[64,2048]{1,0:T(8,128)}) custom-call(bf16[64,4096]{1,0:T(8,128)(2,1)} %bitcast.11, bf16[64,4096]{1,0:T(8,128)(2,1)} %bitcast.12, bf16[64,4096]{1,0:T(8,128)(2,1)} %bitcast.13, bf16[64,4096]{1,0:T(8,128)(2,1)} %table.1, s32[2,128]{1,0:T(2,128)} %bitcast.17, ...), custom_call_target="tpu_custom_call" | custom-call | tf_op jit(solution)/shard_map/pallas_call | solution.py:201
  89.4 0.0 copy-start.1
  89.4 1.9 %copy.15 = bf16[1,64,4096]{2,1,0:T(8,128)(2,1)} copy(bf16[1,64,4096]{2,1,0:T(8,128)(2,1)} %bitcast.10) | data formatting | bytes 1048576
  91.4 0.0 copy-done.1
  91.4 0.0 copy-start.2
  91.4 0.0 copy-start
  91.4 0.8 copy.16
  92.2 0.0 copy-done.2
  92.2 0.6 copy.17
  92.8 0.0 copy-done
  92.8 0.8 copy.18
Async XLA Ops:
  89.4 1.9 %copy-start.1 = (bf16[64,4096]{1,0:T(8,128)(2,1)S(1)}, bf16[64,4096]{1,0:T(8,128)(2,1)}, u32[]{:S(2)}) copy-start(bf16[64,4096]{1,0:T(8,128)(2,1)} %get-tuple-element.9) | copy-start | bytes 1572868
  91.4 0.8 copy-start.2
  91.4 1.4 %copy-start = (f32[64,2048]{1,0:T(8,128)S(1)}, f32[64,2048]{1,0:T(8,128)}, u32[]{:S(2)}) copy-start(f32[64,2048]{1,0:T(8,128)} %get-tuple-element.19) | copy-start | bytes 1572868

commit v4 on v3

--- a/solution.py
+++ b/solution.py
@@ -65,7 +65,9 @@
     gate_a, cot_a, gate_b, table, row_ids, slots, weights,
     mixed_b, grad_gate, grad_weights, grad_table,
     asks, mix_a, asked, rows_out, fetched, grads_out, arrived, grad_memory, scores,
+    table_far, asked_far,
     ask_send, ask_recv, grad_send, grad_recv, row_send, row_recv,
+    table_send, table_recv, far_send, far_recv,
 ):
     sections = lax.axis_size("section")
     owners = lax.axis_size("table")
@@ -75,6 +77,10 @@
     part = features // sections
     everyone = sections * owners
     mine = sec * owners + me
+    half = owners // 2
+    seat = lax.rem(me, half)
+    low = me - seat
+    twin = lax.rem(me + half, owners)
     f32 = jnp.float32
 
     def peers(step, first):
@@ -106,6 +112,15 @@
 
     peers(lambda s, t: remote(asks.at[t], asked.at[mine], ask_send, ask_recv, s, t), 1)
     pltpu.make_async_copy(asks.at[me], asked.at[mine], ask_recv).start()
+
+    @pl.loop(1, half)
+    def _(hop):
+        t = low + lax.rem(seat + hop, half)
+        other = lax.rem(t + half, owners)
+        remote(asks.at[other], asked_far.at[seat], far_send, far_recv, sec, t)
+
+    pltpu.make_async_copy(asks.at[twin], asked_far.at[seat], far_recv).start()
+    remote(table, table_far, table_send, table_recv, sec, twin)
     mix_a[...] = spread(mix_picks(slots[0], weights[0]), wide_a)
 
     @pl.loop(0, features // CHUNK)
@@ -127,20 +142,30 @@
     pltpu.make_async_copy(grads_out.at[sec, me], arrived.at[mine], grad_recv).start()
 
     drain(asked, ask_recv)
-    wanted = asked[pl.ds(sec * owners, owners)].reshape(owners * 2 * ROW_LIMIT, -1)[:, :rows_dev]
-
-    @pl.loop(0, features // CHUNK)
-    def _(c):
-        cols = pl.ds(pl.multiple_of(c * CHUNK, CHUNK), CHUNK)
-        rows = jnp.dot(wanted, table[:, cols], preferred_element_type=f32).astype(jnp.bfloat16)
-        rows_out[:, :, cols] = rows.reshape(owners, 2 * ROW_LIMIT, CHUNK)
-
-    @pl.loop(1, owners)
-    def _(hop):
-        t = lax.rem(me + hop, owners)
-        remote(rows_out.at[t], fetched.at[me], row_send, row_recv, sec, t)
-
-    pltpu.make_async_copy(rows_out.at[me], fetched.at[me], row_recv).start()
+    drain(asked_far, far_recv)
+
+    def serve(wanted, rows_ref, side, place):
+        wanted = wanted.reshape(half * 2 * ROW_LIMIT, -1)[:, :rows_dev]
+
+        @pl.loop(0, features // CHUNK)
+        def _(c):
+            cols = pl.ds(pl.multiple_of(c * CHUNK, CHUNK), CHUNK)
+            rows = jnp.dot(wanted, rows_ref[:, cols], preferred_element_type=f32)
+            rows = rows.astype(jnp.bfloat16).reshape(half, 2 * ROW_LIMIT, CHUNK)
+            rows_out[side, :, :, cols] = rows
+
+        @pl.loop(1, half)
+        def _(hop):
+            spot = lax.rem(seat + hop, half)
+            remote(
+                rows_out.at[side, spot], fetched.at[place], row_send, row_recv, sec, low + spot
+            )
+
+        pltpu.make_async_copy(rows_out.at[side, seat], fetched.at[place], row_recv).start()
+
+    serve(asked[pl.ds(sec * owners + low, half)], table, 0, me)
+    drain(table_far, table_recv)
+    serve(asked_far[...], table_far, 1, twin)
 
     mix_b = spread(mix_picks(slots[1], weights[1]), wide_b)
     asked_a = asked[...].astype(f32)[:, :ROW_LIMIT].reshape(everyone * ROW_LIMIT, -1)
@@ -184,7 +209,9 @@
     grad_weights[...] = jnp.take_along_axis(listed, slots[0], axis=1)
     drain(asked.at[pl.ds(0, everyone - 1)], ask_send)
     drain(arrived.at[pl.ds(0, everyone - 1)], grad_send)
-    drain(rows_out.at[pl.ds(0, owners - 1)], row_send)
+    drain(rows_out.at[:, pl.ds(0, half - 1)], row_send)
+    drain(asked_far.at[pl.ds(0, half - 1)], far_send)
+    drain(table_far, table_send)
 
 
 def local(gate_a, cotangent_a, gate_b, table, row_ids, slots, weights):
@@ -212,14 +239,16 @@
             pltpu.VMEM((owners, 2 * ROW_LIMIT, lanes), bf16),
             pltpu.VMEM((tokens, owners * 2 * ROW_LIMIT), bf16),
             pltpu.VMEM((everyone, 2 * ROW_LIMIT, lanes), bf16),
-            pltpu.VMEM((owners, 2 * ROW_LIMIT, features), bf16),
+            pltpu.VMEM((2, owners // 2, 2 * ROW_LIMIT, features), bf16),
             pltpu.VMEM((owners, 2 * ROW_LIMIT, features), bf16),
             pltpu.VMEM((sections, owners, ROW_LIMIT, part), bf16),
             pltpu.VMEM((everyone, ROW_LIMIT, part), bf16),
             pltpu.VMEM((tokens, features), bf16),
             pltpu.VMEM((tokens, owners * 2 * ROW_LIMIT), jnp.float32),
+            pltpu.VMEM((rows_dev, features), bf16),
+            pltpu.VMEM((owners // 2, 2 * ROW_LIMIT, lanes), bf16),
         ]
-        + [pltpu.SemaphoreType.DMA] * 6,
+        + [pltpu.SemaphoreType.DMA] * 10,
         compiler_params=pltpu.CompilerParams(
             collective_id=0, has_side_effects=True, vmem_limit_bytes=60 * 1024 * 1024
         ),

time: 93.8 us -> 81.1 us (0.86)
  the two profiles are of different devices: /device:TPU:15 before, /device:TPU:7 now
where the time goes in v4:
time: 81.1 us; the launch traced here: 80.9 us
  Pallas kernels  76.2 us (94%)
  local copies, waits for them, and re-layouts  4.14 us (5%)
    pallas_call x1, Pallas kernels, local(): pl.pallas_call(exchange, out_shape=(jax.ShapeDtypeStruct((tokens, feature...  76.2 us
    unnamed x10, local copies, waits for them, and re-layouts  4.14 us

profile of v4, /device:TPU:7, one launch (start us, length us, event | category | flops | bytes accessed | tf_op | source)
XLA Modules:
  0.0 80.9 jit_solution(9933850001445303103)
XLA Ops:
  0.6 76.2 %shard_map.102 = (bf16[64,4096]{1,0:T(8,128)(2,1)}, bf16[64,4096]{1,0:T(8,128)(2,1)}, f32[64,128]{1,0:T(8,128)}, f32[64,2048]{1,0:T(8,128)}) custom-call(bf16[64,4096]{1,0:T(8,128)(2,1)} %bitcast.11, bf16[64,4096]{1,0:T(8,128)(2,1)} %bitcast.12, bf16[64,4096]{1,0:T(8,128)(2,1)} %bitcast.13, bf16[64,4096]{1,0:T(8,128)(2,1)} %table.1, s32[2,128]{1,0:T(2,128)} %bitcast.17, ...), custom_call_target="tpu_custom_call" | custom-call | tf_op jit(solution)/shard_map/pallas_call | solution.py:228
  76.8 0.0 copy-start.1
  76.8 1.9 %copy.15 = bf16[1,64,4096]{2,1,0:T(8,128)(2,1)} copy(bf16[1,64,4096]{2,1,0:T(8,128)(2,1)} %bitcast.10) | data formatting | bytes 1048576
  78.7 0.0 copy-done.1
  78.7 0.0 copy-start.2
  78.7 0.0 copy-start
  78.7 0.8 copy.16
  79.5 0.0 copy-done.2
  79.5 0.6 copy.17
  80.1 0.0 copy-done
  80.1 0.8 copy.18
Async XLA Ops:
  76.8 1.9 %copy-start.1 = (bf16[64,4096]{1,0:T(8,128)(2,1)S(1)}, bf16[64,4096]{1,0:T(8,128)(2,1)}, u32[]{:S(2)}) copy-start(bf16[64,4096]{1,0:T(8,128)(2,1)} %get-tuple-element.9) | copy-start | bytes 1572868
  78.7 0.8 copy-start.2
  78.7 1.4 %copy-start = (f32[64,2048]{1,0:T(8,128)S(1)}, f32[64,2048]{1,0:T(8,128)}, u32[]{:S(2)}) copy-start(f32[64,2048]{1,0:T(8,128)} %get-tuple-element.19) | copy-start | bytes 1572868
